TPU v7x, 32 devices: a whole 2x2x4 slice. The times are simulated.
32 devices in a mesh: dp: 8 (over z, y), mp: 4 (over x, core).
Axes of the slice: x: 2, y: 2, z: 4, core: 2. Of those that a mesh axis runs over, the one named last changes fastest.
Arguments:
- acts: bfloat16 [8192, 2048], P('dp', 'mp'), may hold values from -6 to 6
- out_grads: bfloat16 [2, 28672, 2048], P(None, 'dp', 'mp'), may hold values from -0.125 to 0.125
- proj_old: float32 [2, 8192, 256], P(None, 'dp'), may hold values from -0.0625 to 0.0625
- moment_one: float32 [2, 28672, 256], P(None, 'dp', 'mp'), may hold values from -12 to 12
- moment_two: float32 [2, 28672, 256], P(None, 'dp', 'mp'), may hold values from 1 to 20
Outputs:
- proj_new: float32 [2, 8192, 256], P(None, 'dp')
- first_new: float32 [2, 28672, 256], P(None, 'dp', 'mp')
- second_new: float32 [2, 28672, 256], P(None, 'dp', 'mp')
- step_update: float32 [2, 28672, 256], P(None, 'dp', 'mp')
All inputs are finite; a program needn't handle non-finite values.
Results may differ from a plain program's by a relative error of at most 0.03.
Values may be sent and summed in bfloat16 or wider, within the bound.
A program may use at most 128 MiB of HBM per device.

v0:
```python
import jax
import jax.numpy as jnp
from jax import lax
from jax.sharding import PartitionSpec as P

SWEEPS = 2


def orthonormal(image, gram):
    lower = jnp.linalg.cholesky(gram)
    solved = jax.scipy.linalg.solve_triangular(lower, jnp.swapaxes(image, 1, 2), lower=True)
    return jnp.swapaxes(solved, 1, 2)


def shards(acts, out_grads, proj_old, moment_one, moment_two):

    def grads_fold(piece):
        return jnp.einsum("kft,tkr->kfr", out_grads, piece, preferred_element_type=jnp.float32)

    def token_product(basis):
        basis_half = basis.astype(jnp.bfloat16)
        local = jnp.einsum("dt,kdr->tkr", acts, basis_half, preferred_element_type=jnp.float32)
        share = lax.psum_scatter(local, "dp", scatter_dimension=0, tiled=True).astype(jnp.bfloat16)
        coeff = lax.all_gather(share, "dp", axis=0, tiled=True)
        return grads_fold(coeff)

    basis = proj_old
    for sweep in range(SWEEPS):
        hidden_part = token_product(basis)
        hidden_share = lax.psum_scatter(
            hidden_part.astype(jnp.bfloat16), "mp", scatter_dimension=1, tiled=True
        )
        token_part = jnp.einsum(
            "kft,kfr->tkr",
            out_grads,
            lax.all_gather(hidden_share, "mp", axis=1, tiled=True),
            preferred_element_type=jnp.float32,
        )
        token_share = lax.psum_scatter(token_part, "dp", scatter_dimension=0, tiled=True).astype(
            jnp.bfloat16
        )
        image_part = jnp.einsum(
            "dt,tkr->kdr",
            acts,
            lax.all_gather(token_share, "dp", axis=0, tiled=True),
            preferred_element_type=jnp.float32,
        )
        image = lax.psum(image_part.astype(jnp.bfloat16), "mp").astype(jnp.float32)
        gram_local = jnp.einsum("kdr,kds->krs", image, image, precision=lax.Precision.HIGHEST)
        gram = lax.psum(gram_local, "dp")
        basis = orthonormal(image, gram)
    projected_part = token_product(basis)
    projected = lax.psum_scatter(
        projected_part.astype(jnp.bfloat16), "mp", scatter_dimension=2, tiled=True
    ).astype(jnp.float32)
    first_new = 0.9 * moment_one + 0.1 * projected
    second_new = 0.999 * moment_two + 0.001 * projected * projected
    step_update = first_new / (jnp.sqrt(second_new) + 1e-08)
    return (basis, first_new, second_new, step_update)


def solution(mesh):
    placed = (
        P("dp", "mp"),
        P(None, "dp", "mp"),
        P(None, "dp", None),
        P(None, "dp", "mp"),
        P(None, "dp", "mp"),
    )
    return jax.shard_map(
        shards,
        mesh=mesh,
        in_specs=placed,
        out_specs=(
            P(None, "dp", None),
            P(None, "dp", "mp"),
            P(None, "dp", "mp"),
            P(None, "dp", "mp"),
        ),
        check_vma=False,
    )
```

profile of v0, /device:TPU:0, one launch (start us, length us, event | category | flops | bytes accessed | tf_op | source)
XLA Modules:
  0.0 1283.0 jit_solution(4463060384800956341)
XLA Ops:
  11.5 74.2 %all-reduce.23 = bf16[512,2,256]{2,1,0:T(2,128)(2,1)S(1)} all-reduce(f32[512,2,256]{2,1,0:T(2,128)S(1)} %copy.67), channel_id=2, replica_groups=mesh['dp'=8,'mp'=4] {'dp'}, use_global_device_ids=true, to_apply=%region_0.0.clone | all-reduce | flops 262144 | bytes 1572864
  87.1 31.5 %all_gather.21 = bf16[512,2,256]{2,1,0:T(2,128)(2,1)S(1)} all-gather(bf16[64,2,256]{2,1,0:T(2,128)(2,1)S(1)} %dynamic-slice_convert_fusion.4), channel_id=1, replica_groups=mesh['dp'=8,'mp'=4] {'dp'}, dimensions={0}, use_global_device_ids=true | all-gather | bytes 589824 | tf_op jit(solution)/shard_map/all_gather | solution.py:24
  118.6 7.1 fusion
  125.7 9.9 copy.106
  140.1 40.0 %reduce-scatter.10.cloned.1.call-done = bf16[896,512]{1,0:T(8,128)(2,1)} async-done(((bf16[3584,512]{1,0:T(8,128)(2,1)}), bf16[896,512]{1,0:T(8,128)(2,1)}) %reduce-scatter.10.cloned.1.call-update) | async-done | bytes 917520
  185.2 31.6 %all-gather.3.cloned.1.call-done = bf16[2,3584,256]{1,2,0:T(8,128)(2,1)} async-done(((bf16[2,896,256]{1,2,0:T(8,128)(2,1)}), bf16[2,3584,256]{1,2,0:T(8,128)(2,1)}) %all-gather.3.cloned.1.call-update) | async-done | bytes 3670032 | tf_op jit(solution)/shard_map/all_gather | solution.py:36
  223.6 72.5 %all-reduce.24 = bf16[512,2,256]{2,1,0:T(2,128)(2,1)S(1)} all-reduce(f32[512,2,256]{2,1,0:T(2,128)S(1)} %copy.69), channel_id=4, replica_groups=mesh['dp'=8,'mp'=4] {'dp'}, use_global_device_ids=true, to_apply=%region_2.0.clone | all-reduce | flops 262144 | bytes 1572864
  296.2 31.4 %all_gather.23 = bf16[512,2,256]{2,1,0:T(2,128)(2,1)S(1)} all-gather(bf16[64,2,256]{2,1,0:T(2,128)(2,1)S(1)} %dynamic-slice_convert_fusion.3), channel_id=1, replica_groups=mesh['dp'=8,'mp'=4] {'dp'}, dimensions={0}, use_global_device_ids=true | all-gather | bytes 589824 | tf_op jit(solution)/shard_map/all_gather | solution.py:45
  329.4 33.4 %all-reduce.16.cloned.1.call-done = bf16[2,1024,256]{1,2,0:T(8,128)(2,1)} async-done(((bf16[2,1024,256]{1,2,0:T(8,128)(2,1)}), bf16[2,1024,256]{1,2,0:T(8,128)(2,1)}) %all-reduce.16.cloned.1.call-update) | async-done | bytes 1048592 | tf_op jit(solution)/shard_map/psum | solution.py:48
  367.6 71.9 %all-reduce.18.cloned.1.call-done = f32[2,256,256]{1,2,0:T(8,128)} async-done(((f32[2,256,256]{1,2,0:T(8,128)}), f32[2,256,256]{1,2,0:T(8,128)}) %all-reduce.18.cloned.1.call-update) | async-done | bytes 524304 | tf_op jit(solution)/shard_map/psum | solution.py:50
  442.7 23.5 %custom-call.17 = f32[2,128,128]{2,1,0:T(8,128)S(1)} custom-call(f32[2,128,128]{2,1,0:T(8,128)S(1)} %cholesky.198), custom_call_target="Cholesky" | custom-call | tf_op jit(solution)/shard_map/jit(cholesky)/cholesky | solution.py:10
  466.2 19.7 %custom-call.18 = f32[2,1,128,128]{2,3,1,0:T(8,128)S(1)} custom-call(f32[2,1,128,128]{3,2,1,0:T(8,128)S(1)} %select_bitcast_fusion.1), custom_call_target="InvertDiagBlocksLowerTriangular" | custom-call | tf_op jit(solution)/shard_map/jit(cholesky)/cholesky | solution.py:10
  490.6 24.3 %custom-call.19 = f32[2,128,128]{2,1,0:T(8,128)S(1)} custom-call(f32[2,128,128]{2,1,0:T(8,128)} %convolution_subtract_fusion.3), custom_call_target="Cholesky" | custom-call | tf_op jit(solution)/shard_map/jit(cholesky)/cholesky | solution.py:10
  518.5 7.3 while.4
  525.8 41.1 %custom-call.20 = f32[2,2,128,128]{2,3,1,0:T(8,128)} custom-call(f32[2,2,128,128]{3,2,1,0:T(8,128)} %bitcast.143), custom_call_target="InvertDiagBlocksLowerTriangular" | custom-call | tf_op jit(solution)/shard_map/jit(_solve_triangular)/vmap()/triangular_solve | solution.py:11
  573.2 71.6 %all-reduce.25 = bf16[512,2,256]{2,1,0:T(2,128)(2,1)S(1)} all-reduce(f32[512,2,256]{2,1,0:T(2,128)S(1)} %copy.79), channel_id=5, replica_groups=mesh['dp'=8,'mp'=4] {'dp'}, use_global_device_ids=true, to_apply=%region_9.0.clone | all-reduce | flops 262144 | bytes 1572864
  644.9 31.5 %all_gather.24 = bf16[512,2,256]{2,1,0:T(2,128)(2,1)S(1)} all-gather(bf16[64,2,256]{2,1,0:T(2,128)(2,1)S(1)} %dynamic-slice_convert_fusion.2), channel_id=1, replica_groups=mesh['dp'=8,'mp'=4] {'dp'}, dimensions={0}, use_global_device_ids=true | all-gather | bytes 589824 | tf_op jit(solution)/shard_map/all_gather | solution.py:24
  676.5 7.1 fusion.1
  683.6 9.9 copy.108
  698.0 39.0 %reduce-scatter.12.cloned.1.call-done = bf16[896,512]{1,0:T(8,128)(2,1)} async-done(((bf16[3584,512]{1,0:T(8,128)(2,1)}), bf16[896,512]{1,0:T(8,128)(2,1)}) %reduce-scatter.12.cloned.1.call-update) | async-done | bytes 917520
  742.1 31.4 %all-gather.5.cloned.1.call-done = bf16[2,3584,256]{1,2,0:T(8,128)(2,1)} async-done(((bf16[2,896,256]{1,2,0:T(8,128)(2,1)}), bf16[2,3584,256]{1,2,0:T(8,128)(2,1)}) %all-gather.5.cloned.1.call-update) | async-done | bytes 3670032 | tf_op jit(solution)/shard_map/all_gather | solution.py:36
  780.4 72.5 %all-reduce.26 = bf16[512,2,256]{2,1,0:T(2,128)(2,1)S(1)} all-reduce(f32[512,2,256]{2,1,0:T(2,128)S(1)} %copy.81), channel_id=7, replica_groups=mesh['dp'=8,'mp'=4] {'dp'}, use_global_device_ids=true, to_apply=%region_11.0.clone | all-reduce | flops 262144 | bytes 1572864
  853.0 31.4 %all_gather.26 = bf16[512,2,256]{2,1,0:T(2,128)(2,1)S(1)} all-gather(bf16[64,2,256]{2,1,0:T(2,128)(2,1)S(1)} %dynamic-slice_convert_fusion.1), channel_id=1, replica_groups=mesh['dp'=8,'mp'=4] {'dp'}, dimensions={0}, use_global_device_ids=true | all-gather | bytes 589824 | tf_op jit(solution)/shard_map/all_gather | solution.py:45
  886.2 33.5 %all-reduce.20.cloned.1.call-done = bf16[2,1024,256]{1,2,0:T(8,128)(2,1)} async-done(((bf16[2,1024,256]{1,2,0:T(8,128)(2,1)}), bf16[2,1024,256]{1,2,0:T(8,128)(2,1)}) %all-reduce.20.cloned.1.call-update) | async-done | bytes 1048592 | tf_op jit(solution)/shard_map/psum | solution.py:48
  924.2 72.6 %all-reduce.22.cloned.1.call-done = f32[2,256,256]{1,2,0:T(8,128)} async-done(((f32[2,256,256]{1,2,0:T(8,128)}), f32[2,256,256]{1,2,0:T(8,128)}) %all-reduce.22.cloned.1.call-update) | async-done | bytes 524304 | tf_op jit(solution)/shard_map/psum | solution.py:50
  999.2 23.5 %custom-call.21 = f32[2,128,128]{2,1,0:T(8,128)S(1)} custom-call(f32[2,128,128]{2,1,0:T(8,128)S(1)} %cholesky.201), custom_call_target="Cholesky" | custom-call | tf_op jit(solution)/shard_map/jit(cholesky)/cholesky | solution.py:10
  1022.7 19.7 %custom-call.22 = f32[2,1,128,128]{2,3,1,0:T(8,128)S(1)} custom-call(f32[2,1,128,128]{3,2,1,0:T(8,128)S(1)} %select_bitcast_fusion), custom_call_target="InvertDiagBlocksLowerTriangular" | custom-call | tf_op jit(solution)/shard_map/jit(cholesky)/cholesky | solution.py:10
  1043.1 23.5 %custom-call.23 = f32[2,128,128]{2,1,0:T(8,128)S(1)} custom-call(f32[2,128,128]{2,1,0:T(8,128)S(1)} %convolution_subtract_fusion.2), custom_call_target="Cholesky" | custom-call | tf_op jit(solution)/shard_map/jit(cholesky)/cholesky | solution.py:10
  1071.1 39.5 %custom-call.24 = f32[2,2,128,128]{2,3,1,0:T(8,128)S(1)} custom-call(f32[2,2,128,128]{3,2,1,0:T(8,128)S(1)} %bitcast.142), custom_call_target="InvertDiagBlocksLowerTriangular" | custom-call | tf_op jit(solution)/shard_map/jit(_solve_triangular)/vmap()/triangular_solve | solution.py:11
  1120.1 72.8 %all-reduce.27 = bf16[512,2,256]{2,1,0:T(2,128)(2,1)} all-reduce(f32[512,2,256]{2,1,0:T(2,128)} %copy.91), channel_id=8, replica_groups=mesh['dp'=8,'mp'=4] {'dp'}, use_global_device_ids=true, to_apply=%region_14.17.clone | all-reduce | flops 262144 | bytes 1572864
  1193.8 31.7 %all_gather.27 = bf16[512,2,256]{2,1,0:T(2,128)(2,1)S(1)} all-gather(bf16[64,2,256]{2,1,0:T(2,128)(2,1)S(1)} %dynamic-slice_convert_fusion), channel_id=1, replica_groups=mesh['dp'=8,'mp'=4] {'dp'}, dimensions={0}, use_global_device_ids=true | all-gather | bytes 589824 | tf_op jit(solution)/shard_map/all_gather | solution.py:24
  1237.2 34.3 %reduce-scatter.8.cloned.1.call-done = bf16[2,3584,64]{1,2,0:T(8,128)(2,1)} async-done(((bf16[2,3584,256]{1,2,0:T(8,128)(2,1)}), bf16[2,3584,64]{1,2,0:T(8,128)(2,1)}) %reduce-scatter.8.cloned.1.call-update) | async-done | bytes 917520 | tf_op jit(solution)/shard_map/reduce_scatter | solution.py:53
  (115 shorter events, 114.4 us)
Async XLA Ops:
  7.2 1.2 copy-start
  7.2 173.0 %reduce-scatter.10.cloned.1.call-start = ((), (), s32[]{:S(2)}) async-start(), calls=%async_computation.10 | async-start | bytes 4587520
  10.7 75.1 %copy-start.7 = (u32[32]{0:T(128)S(1)}, u32[32]{0:T(128)}, u32[]{:S(2)}) copy-start(u32[32]{0:T(128)} %constant.98) | copy-start | bytes 388
  140.1 76.7 %all-gather.3.cloned.1.call-start = ((), (), s32[]{:S(2)}) async-start(), calls=%async_computation.3 | async-start | bytes 4587520 | tf_op jit(solution)/shard_map/all_gather | solution.py:36
  185.1 177.7 %all-reduce.16.cloned.1.call-start = ((), (), s32[]{:S(2)}) async-start(), calls=%async_computation.4 | async-start | bytes 2097152 | tf_op jit(solution)/shard_map/psum | solution.py:48
  329.3 110.2 %all-reduce.18.cloned.1.call-start = ((), (), s32[]{:S(2)}) async-start(), calls=%async_computation.5 | async-start | bytes 1048576 | tf_op jit(solution)/shard_map/psum | solution.py:50
  362.9 3.2 copy-start.1
  365.8 371.1 %reduce-scatter.12.cloned.1.call-start = ((), (), s32[]{:S(2)}) async-start(), calls=%async_computation.11 | async-start | bytes 4587520
  441.9 0.8 copy-start.5
  486.7 80.3 %copy-start.3 = (f32[2,256,1024]{2,1,0:T(8,128)S(1)}, f32[2,256,1024]{2,1,0:T(8,128)}, u32[]{:S(2)}) copy-start(f32[2,256,1024]{2,1,0:T(8,128)} %convert_bitcast_fusion.1) | copy-start | bytes 6291460
  568.9 2.0 copy-start.6
  697.9 75.6 %all-gather.5.cloned.1.call-start = ((), (), s32[]{:S(2)}) async-start(), calls=%async_computation.6 | async-start | bytes 4587520 | tf_op jit(solution)/shard_map/all_gather | solution.py:36
  741.9 177.7 %all-reduce.20.cloned.1.call-start = ((), (), s32[]{:S(2)}) async-start(), calls=%async_computation.7 | async-start | bytes 2097152 | tf_op jit(solution)/shard_map/psum | solution.py:48
  886.1 110.7 %all-reduce.22.cloned.1.call-start = ((), (), s32[]{:S(2)}) async-start(), calls=%async_computation.8 | async-start | bytes 1048576 | tf_op jit(solution)/shard_map/psum | solution.py:50
  919.6 3.0 copy-start.2
  922.6 348.9 %reduce-scatter.8.cloned.1.call-start = ((), (), s32[]{:S(2)}) async-start(), calls=%async_computation.9 | async-start | bytes 4587520 | tf_op jit(solution)/shard_map/reduce_scatter | solution.py:53
  1234.0 37.5 %copy-start.4 = (f32[2,3584,64]{1,2,0:T(8,128)S(1)}, f32[2,3584,64]{1,2,0:T(8,128)}, u32[]{:S(2)}) copy-start(f32[2,3584,64]{1,2,0:T(8,128)} %param.12) | copy-start | bytes 5505028
Sparse Core Ops, SparseCore 0:
  140.2 39.8 reduce-scatter.9
  185.3 31.4 all-gather.2
  329.4 33.3 all-reduce.15
  366.7 72.7 all-reduce.17
  698.0 38.8 reduce-scatter.11
  742.0 31.4 all-gather.4
  886.2 33.3 all-reduce.19
  924.0 72.7 all-reduce.21
  1232.7 38.7 reduce-scatter.7
where the time goes:
time: 1290 us; the launch traced here: 1280 us
  blocking collectives  521 us (40%)
  waiting for transfers between devices  388 us (30%)
  other arithmetic  230 us (18%)
  local copies, waits for them, and re-layouts  65.7 us (5%)
  matrix products  62.8 us (5%)
  between operations  15.2 us (1%)
    unnamed x5, blocking collectives  364 us
    psum x2, waiting for transfers between devices, shards(): gram = lax.psum(gram_local, 'dp')  145 us
    another operation x17, other arithmetic, orthonormal(): lower = jnp.linalg.cholesky(gram)  135 us
    all_gather x3, blocking collectives, token_product(): coeff = lax.all_gather(share, 'dp', axis=0, tiled=True)  94.8 us
    another operation x6, other arithmetic, orthonormal(): jax.scipy.linalg.solve_triangular(lower, jnp.swapaxes(image, 1, 2), lower...  82.8 us
    unnamed x11, waiting for transfers between devices  79.1 us
    psum x2, waiting for transfers between devices, shards(): image = lax.psum(image_part.astype(jnp.bfloat16), 'mp').astype(jnp.float32)  66.9 us
    all_gather x2, waiting for transfers between devices, shards(): lax.all_gather(hidden_share, 'mp', axis=1, tiled=True)  63 us
  transfers between devices with their start and end apart: 9, of which 9 were waited for; matrix products, arithmetic and copies ran while one was open for 1% of the time, Pallas kernels for 0%

commit v1 on v0

--- a/solution.py
+++ b/solution.py
@@ -47,7 +47,9 @@
         )
         image = lax.psum(image_part.astype(jnp.bfloat16), "mp").astype(jnp.float32)
         gram_local = jnp.einsum("kdr,kds->krs", image, image, precision=lax.Precision.HIGHEST)
-        gram = lax.psum(gram_local, "dp")
+        gram = gram_local
+        for hop in (1, 2, 4):
+            gram = gram + lax.ppermute(gram, "dp", [(dev, dev ^ hop) for dev in range(8)])
         basis = orthonormal(image, gram)
     projected_part = token_product(basis)
     projected = lax.psum_scatter(

time: 1290 us -> 1240 us (0.961)
  waiting for transfers between devices: 388 us -> 332 us
    psum x2 -> x0, waiting for transfers between devices: 145 us -> none  [shards(): gram = lax.psum(gram_local, 'dp')]
    ppermute x0 -> x6, waiting for transfers between devices: none -> 87 us  [shards(): lax.ppermute(gram, 'dp', [(dev, dev ^ hop) for dev in range(8)])]
    unnamed x11 -> x9, waiting for transfers between devices: 79.1 us -> 79.8 us
  transfers between devices with their start and end apart: 9 -> 13, of which waited for: 9 -> 13; matrix products, arithmetic and copies ran while one was open for 1% -> 1% of each run, Pallas kernels for 0% -> 0%
where the time goes in v1:
time: 1240 us; the launch traced here: 1230 us
  blocking collectives  522 us (42%)
  waiting for transfers between devices  332 us (27%)
  other arithmetic  228 us (18%)
  local copies, waits for them, and re-layouts  63.4 us (5%)
  matrix products  61 us (5%)
  between operations  15.5 us (1%)
    unnamed x5, blocking collectives  364 us
    another operation x17, other arithmetic, orthonormal(): lower = jnp.linalg.cholesky(gram)  135 us
    all_gather x3, blocking collectives, token_product(): coeff = lax.all_gather(share, 'dp', axis=0, tiled=True)  94.6 us
    ppermute x6, waiting for transfers between devices, shards(): lax.ppermute(gram, 'dp', [(dev, dev ^ hop) for dev in range(8)])  87 us
    another operation x6, other arithmetic, orthonormal(): jax.scipy.linalg.solve_triangular(lower, jnp.swapaxes(image, 1, 2), lower...  82.8 us
    unnamed x9, waiting for transfers between devices  79.8 us
    psum x2, waiting for transfers between devices, shards(): image = lax.psum(image_part.astype(jnp.bfloat16), 'mp').astype(jnp.float32)  66.5 us
    all_gather x2, waiting for transfers between devices, shards(): lax.all_gather(hidden_share, 'mp', axis=1, tiled=True)  63.2 us
  transfers between devices with their start and end apart: 13, of which 13 were waited for; matrix products, arithmetic and copies ran while one was open for 1% of the time, Pallas kernels for 0%

profile of v1, /device:TPU:0, one launch (start us, length us, event | category | flops | bytes accessed | tf_op | source)
XLA Modules:
  0.0 1231.3 jit_solution(15317611337338715087)
XLA Ops:
  11.5 74.2 %all-reduce.17 = bf16[512,2,256]{2,1,0:T(2,128)(2,1)S(1)} all-reduce(f32[512,2,256]{2,1,0:T(2,128)S(1)} %copy.73), channel_id=2, replica_groups=mesh['dp'=8,'mp'=4] {'dp'}, use_global_device_ids=true, to_apply=%region_0.0.clone | all-reduce | flops 262144 | bytes 1572864
  87.1 31.5 %all_gather.21 = bf16[512,2,256]{2,1,0:T(2,128)(2,1)S(1)} all-gather(bf16[64,2,256]{2,1,0:T(2,128)(2,1)S(1)} %dynamic-slice_convert_fusion.4), channel_id=1, replica_groups=mesh['dp'=8,'mp'=4] {'dp'}, dimensions={0}, use_global_device_ids=true | all-gather | bytes 589824 | tf_op jit(solution)/shard_map/all_gather | solution.py:24
  125.7 9.9 copy.114
  140.1 40.0 %reduce-scatter.10.cloned.1.call-done = bf16[896,512]{1,0:T(8,128)(2,1)} async-done(((bf16[3584,512]{1,0:T(8,128)(2,1)}), bf16[896,512]{1,0:T(8,128)(2,1)}) %reduce-scatter.10.cloned.1.call-update) | async-done | bytes 917520
  185.2 31.6 %all-gather.3.cloned.1.call-done = bf16[2,3584,256]{1,2,0:T(8,128)(2,1)} async-done(((bf16[2,896,256]{1,2,0:T(8,128)(2,1)}), bf16[2,3584,256]{1,2,0:T(8,128)(2,1)}) %all-gather.3.cloned.1.call-update) | async-done | bytes 3670032 | tf_op jit(solution)/shard_map/all_gather | solution.py:36
  223.6 72.5 %all-reduce.18 = bf16[512,2,256]{2,1,0:T(2,128)(2,1)S(1)} all-reduce(f32[512,2,256]{2,1,0:T(2,128)S(1)} %copy.75), channel_id=4, replica_groups=mesh['dp'=8,'mp'=4] {'dp'}, use_global_device_ids=true, to_apply=%region_2.0.clone | all-reduce | flops 262144 | bytes 1572864
  296.2 31.4 %all_gather.23 = bf16[512,2,256]{2,1,0:T(2,128)(2,1)S(1)} all-gather(bf16[64,2,256]{2,1,0:T(2,128)(2,1)S(1)} %dynamic-slice_convert_fusion.3), channel_id=1, replica_groups=mesh['dp'=8,'mp'=4] {'dp'}, dimensions={0}, use_global_device_ids=true | all-gather | bytes 589824 | tf_op jit(solution)/shard_map/all_gather | solution.py:45
  329.6 33.3 %all-reduce.14.cloned.1.call-done = bf16[2,1024,256]{1,2,0:T(8,128)(2,1)} async-done(((bf16[2,1024,256]{1,2,0:T(8,128)(2,1)}), bf16[2,1024,256]{1,2,0:T(8,128)(2,1)}) %all-reduce.14.cloned.1.call-update) | async-done | bytes 1048592 | tf_op jit(solution)/shard_map/psum | solution.py:48
  366.4 12.0 collective-permute-done
  379.8 11.3 collective-permute-done.1
  394.7 20.2 %collective-permute-done.2 = f32[2,256,256]{1,2,0:T(8,128)S(1)} collective-permute-done((f32[2,256,256]{1,2,0:T(8,128)S(1)}, f32[2,256,256]{1,2,0:T(8,128)S(1)}, u32[]{:S(2)}, u32[]{:S(2)}) %collective-permute-start.2) | collective-permute-done | bytes 524320 | tf_op jit(solution)/shard_map/ppermute | solution.py:52
  416.1 23.5 %custom-call.17 = f32[2,128,128]{2,1,0:T(8,128)S(1)} custom-call(f32[2,128,128]{2,1,0:T(8,128)S(1)} %cholesky.198), custom_call_target="Cholesky" | custom-call | tf_op jit(solution)/shard_map/jit(cholesky)/cholesky | solution.py:10
  439.6 19.7 %custom-call.18 = f32[2,1,128,128]{2,3,1,0:T(8,128)S(1)} custom-call(f32[2,1,128,128]{3,2,1,0:T(8,128)S(1)} %select_bitcast_fusion.1), custom_call_target="InvertDiagBlocksLowerTriangular" | custom-call | tf_op jit(solution)/shard_map/jit(cholesky)/cholesky | solution.py:10
  464.1 24.3 %custom-call.19 = f32[2,128,128]{2,1,0:T(8,128)S(1)} custom-call(f32[2,128,128]{2,1,0:T(8,128)} %slice_subtract_fusion.1), custom_call_target="Cholesky" | custom-call | tf_op jit(solution)/shard_map/jit(cholesky)/cholesky | solution.py:10
  499.2 41.1 %custom-call.20 = f32[2,2,128,128]{2,3,1,0:T(8,128)} custom-call(f32[2,2,128,128]{3,2,1,0:T(8,128)} %bitcast.143), custom_call_target="InvertDiagBlocksLowerTriangular" | custom-call | tf_op jit(solution)/shard_map/jit(_solve_triangular)/vmap()/triangular_solve | solution.py:11
  546.7 72.1 %all-reduce.19 = bf16[512,2,256]{2,1,0:T(2,128)(2,1)S(1)} all-reduce(f32[512,2,256]{2,1,0:T(2,128)S(1)} %copy.86), channel_id=5, replica_groups=mesh['dp'=8,'mp'=4] {'dp'}, use_global_device_ids=true, to_apply=%region_8.0.clone | all-reduce | flops 262144 | bytes 1572864
  618.9 31.3 %all_gather.24 = bf16[512,2,256]{2,1,0:T(2,128)(2,1)S(1)} all-gather(bf16[64,2,256]{2,1,0:T(2,128)(2,1)S(1)} %dynamic-slice_convert_fusion.2), channel_id=1, replica_groups=mesh['dp'=8,'mp'=4] {'dp'}, dimensions={0}, use_global_device_ids=true | all-gather | bytes 589824 | tf_op jit(solution)/shard_map/all_gather | solution.py:24
  671.7 39.7 %reduce-scatter.12.cloned.1.call-done = bf16[896,512]{1,0:T(8,128)(2,1)} async-done(((bf16[3584,512]{1,0:T(8,128)(2,1)}), bf16[896,512]{1,0:T(8,128)(2,1)}) %reduce-scatter.12.cloned.1.call-update) | async-done | bytes 917520
  716.4 31.6 %all-gather.5.cloned.1.call-done = bf16[2,3584,256]{1,2,0:T(8,128)(2,1)} async-done(((bf16[2,896,256]{1,2,0:T(8,128)(2,1)}), bf16[2,3584,256]{1,2,0:T(8,128)(2,1)}) %all-gather.5.cloned.1.call-update) | async-done | bytes 3670032 | tf_op jit(solution)/shard_map/all_gather | solution.py:36
  754.9 72.5 %all-reduce.20 = bf16[512,2,256]{2,1,0:T(2,128)(2,1)S(1)} all-reduce(f32[512,2,256]{2,1,0:T(2,128)S(1)} %copy.88), channel_id=7, replica_groups=mesh['dp'=8,'mp'=4] {'dp'}, use_global_device_ids=true, to_apply=%region_10.13.clone | all-reduce | flops 262144 | bytes 1572864
  827.4 31.4 %all_gather.26 = bf16[512,2,256]{2,1,0:T(2,128)(2,1)S(1)} all-gather(bf16[64,2,256]{2,1,0:T(2,128)(2,1)S(1)} %dynamic-slice_convert_fusion.1), channel_id=1, replica_groups=mesh['dp'=8,'mp'=4] {'dp'}, dimensions={0}, use_global_device_ids=true | all-gather | bytes 589824 | tf_op jit(solution)/shard_map/all_gather | solution.py:45
  860.8 33.2 %all-reduce.16.cloned.1.call-done = bf16[2,1024,256]{1,2,0:T(8,128)(2,1)} async-done(((bf16[2,1024,256]{1,2,0:T(8,128)(2,1)}), bf16[2,1024,256]{1,2,0:T(8,128)(2,1)}) %all-reduce.16.cloned.1.call-update) | async-done | bytes 1048592 | tf_op jit(solution)/shard_map/psum | solution.py:48
  897.6 12.0 collective-permute-done.3
  911.0 11.3 collective-permute-done.4
  925.9 20.3 %collective-permute-done.5 = f32[2,256,256]{1,2,0:T(8,128)S(1)} collective-permute-done((f32[2,256,256]{1,2,0:T(8,128)S(1)}, f32[2,256,256]{1,2,0:T(8,128)S(1)}, u32[]{:S(2)}, u32[]{:S(2)}) %collective-permute-start.5) | collective-permute-done | bytes 524320 | tf_op jit(solution)/shard_map/ppermute | solution.py:52
  946.5 23.5 %custom-call.21 = f32[2,128,128]{2,1,0:T(8,128)S(1)} custom-call(f32[2,128,128]{2,1,0:T(8,128)S(1)} %cholesky.201), custom_call_target="Cholesky" | custom-call | tf_op jit(solution)/shard_map/jit(cholesky)/cholesky | solution.py:10
  970.0 19.7 %custom-call.22 = f32[2,1,128,128]{2,3,1,0:T(8,128)S(1)} custom-call(f32[2,1,128,128]{3,2,1,0:T(8,128)S(1)} %select_bitcast_fusion), custom_call_target="InvertDiagBlocksLowerTriangular" | custom-call | tf_op jit(solution)/shard_map/jit(cholesky)/cholesky | solution.py:10
  990.4 23.5 %custom-call.23 = f32[2,128,128]{2,1,0:T(8,128)S(1)} custom-call(f32[2,128,128]{2,1,0:T(8,128)S(1)} %slice_subtract_fusion), custom_call_target="Cholesky" | custom-call | tf_op jit(solution)/shard_map/jit(cholesky)/cholesky | solution.py:10
  1018.4 39.5 %custom-call.24 = f32[2,2,128,128]{2,3,1,0:T(8,128)S(1)} custom-call(f32[2,2,128,128]{3,2,1,0:T(8,128)S(1)} %bitcast.142), custom_call_target="InvertDiagBlocksLowerTriangular" | custom-call | tf_op jit(solution)/shard_map/jit(_solve_triangular)/vmap()/triangular_solve | solution.py:11
  1067.4 72.9 %all-reduce.21 = bf16[512,2,256]{2,1,0:T(2,128)(2,1)} all-reduce(f32[512,2,256]{2,1,0:T(2,128)} %copy.99), channel_id=8, replica_groups=mesh['dp'=8,'mp'=4] {'dp'}, use_global_device_ids=true, to_apply=%region_12.15.clone | all-reduce | flops 262144 | bytes 1572864
  1141.2 31.7 %all_gather.27 = bf16[512,2,256]{2,1,0:T(2,128)(2,1)S(1)} all-gather(bf16[64,2,256]{2,1,0:T(2,128)(2,1)S(1)} %dynamic-slice_convert_fusion), channel_id=1, replica_groups=mesh['dp'=8,'mp'=4] {'dp'}, dimensions={0}, use_global_device_ids=true | all-gather | bytes 589824 | tf_op jit(solution)/shard_map/all_gather | solution.py:24
  1184.5 35.0 %reduce-scatter.8.cloned.1.call-done = bf16[2,3584,64]{1,2,0:T(8,128)(2,1)} async-done(((bf16[2,3584,256]{1,2,0:T(8,128)(2,1)}), bf16[2,3584,64]{1,2,0:T(8,128)(2,1)}) %reduce-scatter.8.cloned.1.call-update) | async-done | bytes 917520 | tf_op jit(solution)/shard_map/reduce_scatter | solution.py:55
  (127 shorter events, 149.6 us)
Async XLA Ops:
  7.2 1.2 copy-start
  7.2 173.0 %reduce-scatter.10.cloned.1.call-start = ((), (), s32[]{:S(2)}) async-start(), calls=%async_computation.8 | async-start | bytes 4587520
  10.7 75.1 %copy-start.7 = (u32[32]{0:T(128)S(1)}, u32[32]{0:T(128)}, u32[]{:S(2)}) copy-start(u32[32]{0:T(128)} %constant.98) | copy-start | bytes 388
  140.1 76.7 %all-gather.3.cloned.1.call-start = ((), (), s32[]{:S(2)}) async-start(), calls=%async_computation.3 | async-start | bytes 4587520 | tf_op jit(solution)/shard_map/all_gather | solution.py:36
  185.1 177.7 %all-reduce.14.cloned.1.call-start = ((), (), s32[]{:S(2)}) async-start(), calls=%async_computation.4 | async-start | bytes 2097152 | tf_op jit(solution)/shard_map/psum | solution.py:48
  329.3 382.1 %reduce-scatter.12.cloned.1.call-start = ((), (), s32[]{:S(2)}) async-start(), calls=%async_computation.9 | async-start | bytes 4587520
  364.9 28.3 %copy-start.1 = (bf16[2,1024,256]{1,2,0:T(8,128)(2,1)S(1)}, bf16[2,1024,256]{1,2,0:T(8,128)(2,1)}, u32[]{:S(2)}) copy-start(bf16[2,1024,256]{1,2,0:T(8,128)(2,1)} %all-reduce.14.cloned.1.call-done) | copy-start | bytes 3145732
  364.9 13.5 %collective-permute-start = (f32[2,256,256]{1,2,0:T(8,128)S(1)}, f32[2,256,256]{1,2,0:T(8,128)S(1)}, u32[]{:S(2)}, u32[]{:S(2)}) collective-permute-start(f32[2,256,256]{1,2,0:T(8,128)S(1)} %fusion.43), channel_id=1, source_target_pairs={{0,4},{4,0},{8,12},{12,8},{16,20},{20,16},{24,28},{28,24},{1,5},{5... | collective-permute-start | bytes 1572872 | tf_op jit(solution)/shard_map/ppermute | solution.py:52
  378.5 12.6 %collective-permute-start.1 = (f32[2,256,256]{1,2,0:T(8,128)S(1)}, f32[2,256,256]{1,2,0:T(8,128)S(1)}, u32[]{:S(2)}, u32[]{:S(2)}) collective-permute-start(f32[2,256,256]{1,2,0:T(8,128)S(1)} %add.68), channel_id=1, source_target_pairs={{0,8},{4,12},{8,0},{12,4},{16,24},{20,28},{24,16},{28,20},{1,9},{5... | collective-permute-start | bytes 1572872 | tf_op jit(solution)/shard_map/ppermute | solution.py:52
  391.1 23.8 %collective-permute-start.2 = (f32[2,256,256]{1,2,0:T(8,128)S(1)}, f32[2,256,256]{1,2,0:T(8,128)S(1)}, u32[]{:S(2)}, u32[]{:S(2)}) collective-permute-start(f32[2,256,256]{1,2,0:T(8,128)S(1)} %add.69), channel_id=1, source_target_pairs={{0,16},{4,20},{8,24},{12,28},{16,0},{20,4},{24,8},{28,12},{1,17},{... | collective-permute-start | bytes 1572872 | tf_op jit(solution)/shard_map/ppermute | solution.py:52
  415.3 0.8 copy-start.5
  460.1 80.3 %copy-start.3 = (f32[2,256,1024]{2,1,0:T(8,128)S(1)}, f32[2,256,1024]{2,1,0:T(8,128)}, u32[]{:S(2)}) copy-start(f32[2,256,1024]{2,1,0:T(8,128)} %convert_bitcast_fusion.1) | copy-start | bytes 6291460
  542.3 2.0 copy-start.6
  671.7 76.4 %all-gather.5.cloned.1.call-start = ((), (), s32[]{:S(2)}) async-start(), calls=%async_computation.5 | async-start | bytes 4587520 | tf_op jit(solution)/shard_map/all_gather | solution.py:36
  716.4 177.7 %all-reduce.16.cloned.1.call-start = ((), (), s32[]{:S(2)}) async-start(), calls=%async_computation.6 | async-start | bytes 2097152 | tf_op jit(solution)/shard_map/psum | solution.py:48
  860.6 358.9 %reduce-scatter.8.cloned.1.call-start = ((), (), s32[]{:S(2)}) async-start(), calls=%async_computation.7 | async-start | bytes 4587520 | tf_op jit(solution)/shard_map/reduce_scatter | solution.py:55
  896.1 28.2 %copy-start.2 = (bf16[2,1024,256]{1,2,0:T(8,128)(2,1)S(1)}, bf16[2,1024,256]{1,2,0:T(8,128)(2,1)}, u32[]{:S(2)}) copy-start(bf16[2,1024,256]{1,2,0:T(8,128)(2,1)} %all-reduce.16.cloned.1.call-done) | copy-start | bytes 3145732
  896.1 13.5 %collective-permute-start.3 = (f32[2,256,256]{1,2,0:T(8,128)S(1)}, f32[2,256,256]{1,2,0:T(8,128)S(1)}, u32[]{:S(2)}, u32[]{:S(2)}) collective-permute-start(f32[2,256,256]{1,2,0:T(8,128)S(1)} %fusion.44), channel_id=1, source_target_pairs={{0,4},{4,0},{8,12},{12,8},{16,20},{20,16},{24,28},{28,24},{1,5},{5... | collective-permute-start | bytes 1572872 | tf_op jit(solution)/shard_map/ppermute | solution.py:52
  909.7 12.6 %collective-permute-start.4 = (f32[2,256,256]{1,2,0:T(8,128)S(1)}, f32[2,256,256]{1,2,0:T(8,128)S(1)}, u32[]{:S(2)}, u32[]{:S(2)}) collective-permute-start(f32[2,256,256]{1,2,0:T(8,128)S(1)} %add.71), channel_id=1, source_target_pairs={{0,8},{4,12},{8,0},{12,4},{16,24},{20,28},{24,16},{28,20},{1,9},{5... | collective-permute-start | bytes 1572872 | tf_op jit(solution)/shard_map/ppermute | solution.py:52
  922.3 23.8 %collective-permute-start.5 = (f32[2,256,256]{1,2,0:T(8,128)S(1)}, f32[2,256,256]{1,2,0:T(8,128)S(1)}, u32[]{:S(2)}, u32[]{:S(2)}) collective-permute-start(f32[2,256,256]{1,2,0:T(8,128)S(1)} %add.72), channel_id=1, source_target_pairs={{0,16},{4,20},{8,24},{12,28},{16,0},{20,4},{24,8},{28,12},{1,17},{... | collective-permute-start | bytes 1572872 | tf_op jit(solution)/shard_map/ppermute | solution.py:52
  1181.5 38.0 %copy-start.4 = (f32[2,3584,64]{1,2,0:T(8,128)S(1)}, f32[2,3584,64]{1,2,0:T(8,128)}, u32[]{:S(2)}) copy-start(f32[2,3584,64]{1,2,0:T(8,128)} %param.12) | copy-start | bytes 5505028
Sparse Core Ops, SparseCore 0:
  140.2 39.8 reduce-scatter.9
  185.3 31.4 all-gather.2
  329.4 33.3 all-reduce.13
  671.8 39.5 reduce-scatter.11
  716.5 31.4 all-gather.4
  860.7 33.2 all-reduce.15
  1180.1 39.3 reduce-scatter.7
